TPU v7x, 32 devices: a whole 2x2x4 slice. The times are simulated.
32 devices in a mesh: ctx: 8 (over z, y), mp: 4 (over x, core).
Axes of the slice: x: 2, y: 2, z: 4, core: 2. Of those that a mesh axis runs over, the one named last changes fastest.
Arguments:
- query: bfloat16 [32, 8, 8, 128], P(('ctx', 'mp')), may hold values from -8 to 8
- keys: bfloat16 [32, 8, 2048, 128], P(('ctx', 'mp')), may hold values from -5 to 5
- values: bfloat16 [32, 8, 2048, 128], P(('ctx', 'mp')), may hold values from -6 to 6
- chosen: int32 [8, 32, 16], replicated, may hold values from 0 to 31, all different within a row; in each aligned block of 32 rows (0 to 31, 32 to 63, ..., all dimensions but the last counted through in order) at most 32 rows name the same one
- residual: bfloat16 [32, 8192], P('ctx', 'mp'), may hold values from -1.5 to 1.5
- output_weight: bfloat16 [8192, 8192], P('ctx', 'mp'), may hold values from -0.0625 to 0.0625
- norm_gain: float32 [8192], P('mp'), may hold values from 0.5 to 1.5
- gate_weight: bfloat16 [8192, 14336], P('mp', 'ctx'), may hold values from -0.0625 to 0.0625
- up_weight: bfloat16 [8192, 14336], P('mp', 'ctx'), may hold values from -0.0625 to 0.0625
- down_weight: bfloat16 [14336, 8192], P('ctx', 'mp'), may hold values from -0.046875 to 0.046875
Outputs:
- stream: bfloat16 [32, 8192], P('ctx', 'mp')
- update: bfloat16 [32, 8192], P('ctx', 'mp')
Inputs may be any that keep to these rules, and one draw needn't show every extreme that they name: `chosen`: for each KV head, each row lists 16 different partitions; no partition is listed by more than 32 rows of one KV head, and in every draw some partition is listed by exactly 32 rows of some KV head.
All inputs are finite; a program needn't handle non-finite values.
Results may differ from a plain program's by a relative error of at most 0.025.
Values may be sent and summed in bfloat16 or wider, within the bound.
No kernel may reach another device: no remote copies, remote signals or barrier semaphores. Data moves between devices by JAX's collectives and lax.ppermute only.
A program may use at most 128 MiB of HBM per device.

v0:
```python
import jax
import jax.numpy as jnp
from jax import lax
from jax.sharding import PartitionSpec as P

MODEL_WIDTH = 8192
KEPT_PARTITIONS = 16
ROW_DEV = 1
norm_eps = 1e-05
lowest_value = -1e30


def find_slots(listed, target, capacity):
    member = jnp.any(listed == target, axis=2)
    places = jnp.cumsum(member.astype(jnp.int32), axis=1) - 1
    live_count = jnp.sum(member.astype(jnp.int32), axis=1)
    slot_ranks = jnp.arange(capacity, dtype=jnp.int32)
    slot_hits = member[:, :, None] & (places[:, :, None] == slot_ranks[None, None, :])
    row_numbers = jnp.arange(listed.shape[1], dtype=jnp.int32)
    slot_rows = jnp.sum(jnp.where(slot_hits, row_numbers[None, :, None], 0), axis=1)
    slot_valid = slot_ranks[None, :] < live_count[:, None]
    return (slot_rows, slot_valid)


def global_scaling(block_max, block_sum, block_value, slot_rows, slot_valid, all_rows, head_ids):
    kv_heads, capacity, group_size = block_max.shape
    valid_wide = slot_valid[:, :, None]
    max_table = jnp.full((all_rows, kv_heads, group_size), lowest_value, jnp.float32)
    max_table = max_table.at[slot_rows, head_ids[:, None]].max(
        jnp.where(valid_wide, block_max, lowest_value)
    )
    row_top = lax.pmax(max_table.astype(jnp.bfloat16), ("ctx", "mp")).astype(max_table.dtype)
    factor = jnp.where(valid_wide, jnp.exp(block_max - row_top[slot_rows, head_ids[:, None]]), 0.0)
    return (block_value * factor[..., None], block_sum * factor)


def to_owners(array, kv_heads, capacity, per_head, ctx_count):
    shaped = array.reshape(kv_heads, capacity, per_head, -1)
    return jnp.transpose(shaped, (0, 2, 1, 3)).reshape(ctx_count, capacity, -1)


def per_device(
    query,
    keys,
    values,
    chosen,
    residual,
    output_weight,
    norm_gain,
    gate_weight,
    up_weight,
    down_weight,
):
    kv_heads = query.shape[1]
    group_size = query.shape[2]
    head_dim = query.shape[3]
    score_scale = head_dim ** (-0.5)
    ctx_count = lax.axis_size("ctx")
    mp_count = lax.axis_size("mp")
    ctx_place = lax.axis_index("ctx")
    mp_place = lax.axis_index("mp")
    own_part = ctx_place * mp_count + mp_place
    all_queries = lax.all_gather(query, ("ctx", "mp"), axis=0, tiled=True)
    all_rows = all_queries.shape[0]
    capacity = min(4 * ROW_DEV * KEPT_PARTITIONS, all_rows)
    slot_rows, slot_valid = find_slots(chosen, own_part, capacity)
    head_ids = jnp.arange(kv_heads, dtype=jnp.int32)
    picked = all_queries[slot_rows, head_ids[:, None]].reshape(
        kv_heads, capacity * group_size, head_dim
    )

    def attend(inputs):
        query_block, key_block, value_block = inputs
        scores = (
            lax.dot_general(
                query_block, key_block, (((1,), (1,)), ((), ())), preferred_element_type=jnp.float32
            )
            * score_scale
        )
        block_max = jnp.max(scores, axis=1)
        probs = jnp.exp(scores - block_max[:, None])
        block_sum = jnp.sum(probs, axis=1)
        block_value = jnp.dot(
            probs.astype(jnp.bfloat16), value_block, preferred_element_type=jnp.float32
        )
        return (block_max, block_sum, block_value)

    block_max, block_sum, block_value = lax.map(attend, (picked, keys[0], values[0]))
    block_max = block_max.reshape(kv_heads, capacity, group_size)
    block_sum = block_sum.reshape(kv_heads, capacity, group_size)
    block_value = block_value.reshape(kv_heads, capacity, group_size, head_dim)
    per_head = ctx_count // kv_heads
    feat_width = kv_heads * group_size * head_dim // ctx_count
    head_share = kv_heads * group_size // ctx_count
    own_head = ctx_place // per_head
    head_lists = lax.dynamic_index_in_dim(chosen, own_head, 0, keepdims=True)
    sources = jnp.arange(ctx_count, dtype=jnp.int32) * mp_count + mp_place
    source_rows = jax.vmap(lambda source: find_slots(head_lists, source, capacity)[0])(sources)[
        :, 0
    ]
    weighted, scaled_sum = global_scaling(
        block_max, block_sum, block_value, slot_rows, slot_valid, all_rows, head_ids
    )
    send_values = to_owners(weighted, kv_heads, capacity, per_head, ctx_count)
    send_sums = to_owners(scaled_sum, kv_heads, capacity, per_head, ctx_count)
    got_values, got_sums = (
        lax.all_to_all(
            send_values.astype(jnp.bfloat16), "ctx", split_axis=0, concat_axis=0, tiled=True
        ).astype(send_values.dtype),
        lax.all_to_all(
            send_sums.astype(jnp.bfloat16), "ctx", split_axis=0, concat_axis=0, tiled=True
        ).astype(send_sums.dtype),
    )
    numerator = jnp.zeros((all_rows, feat_width), jnp.float32).at[source_rows].add(got_values)
    denominator = jnp.zeros((all_rows, head_share), jnp.float32).at[source_rows].add(got_sums)
    numerator, denominator = (
        lax.psum(numerator.astype(jnp.bfloat16), "mp").astype(jnp.float32),
        lax.psum(denominator.astype(jnp.bfloat16), "mp").astype(jnp.float32),
    )
    attended = (
        (numerator.reshape(all_rows, -1, head_dim) / denominator[:, :, None])
        .reshape(all_rows, -1)
        .astype(jnp.bfloat16)
    )
    rows_here = attended
    projected = lax.psum_scatter(
        jnp.dot(rows_here, output_weight, preferred_element_type=jnp.float32),
        "ctx",
        scatter_dimension=0,
        tiled=True,
    )
    stream = (residual.astype(jnp.float32) + projected).astype(jnp.bfloat16)
    stream_wide = stream.astype(jnp.float32)
    squares = lax.psum(jnp.sum(stream_wide * stream_wide, axis=1), "mp")
    normed = (
        stream_wide * lax.rsqrt(squares / MODEL_WIDTH + norm_eps)[:, None] * norm_gain
    ).astype(jnp.bfloat16)
    row_piece = lax.all_gather(normed, "ctx", axis=0, tiled=True)
    gate_piece = jnp.dot(row_piece, gate_weight, preferred_element_type=jnp.float32)
    up_piece = jnp.dot(row_piece, up_weight, preferred_element_type=jnp.float32)
    gate_up = jnp.stack([gate_piece, up_piece], axis=1)
    gate_up = lax.psum(gate_up.astype(jnp.bfloat16), "mp").astype(jnp.float32)
    hidden = (jax.nn.silu(gate_up[:, 0]) * gate_up[:, 1]).astype(jnp.bfloat16)
    rows_here = hidden
    update = lax.psum_scatter(
        jnp.dot(rows_here, down_weight, preferred_element_type=jnp.float32),
        "ctx",
        scatter_dimension=0,
        tiled=True,
    ).astype(jnp.bfloat16)
    return (stream, update)


def solution(mesh):
    return jax.shard_map(
        per_device,
        mesh=mesh,
        in_specs=(
            P(("ctx", "mp"), None, None, None),
            P(("ctx", "mp"), None, None, None),
            P(("ctx", "mp"), None, None, None),
            P(),
            P("ctx", "mp"),
            P("ctx", "mp"),
            P("mp"),
            P("mp", "ctx"),
            P("mp", "ctx"),
            P("ctx", "mp"),
        ),
        out_specs=(P("ctx", "mp"), P("ctx", "mp")),
        check_vma=False,
    )
```

profile of v0, /device:TPU:0, one launch (start us, length us, event | category | flops | bytes accessed | tf_op | source)
XLA Modules:
  0.0 393.7 jit_solution(18156708375648113719)
XLA Ops:
  7.2 0.9 compare_reduce_fusion
  8.6 44.9 %all_gather.6 = bf16[32,8,8,128]{3,2,1,0:T(8,128)(2,1)S(1)} all-gather(bf16[1,8,8,128]{3,2,1,0:T(8,128)(2,1)} %param.12), channel_id=1, replica_groups=mesh['ctx'=8,'mp'=4] {'ctx','mp'}, dimensions={0}, use_global_device_ids=true | all-gather | bytes 540672 | tf_op jit(solution)/shard_map/all_gather | solution.py:63
  53.5 1.1 gather_fusion
  54.7 29.4 %while.14 = (s32[]{:T(128)}, f32[8,256]{1,0:T(8,128)S(1)}, f32[8,256]{1,0:T(8,128)S(1)}, f32[8,256,128]{2,1,0:T(8,128)S(1)}, bf16[8,256,128]{2,1,0:T(8,128)(2,1)...) while((s32[]{:T(128)}, f32[8,256]{1,0:T(8,128)S(1)}, ...), condition=%wide.region_9.10_spmd, body=%wide.region_6.9_spmd.sunk | while | flops 271580672 | bytes 7546981 | solution.py:88
  54.7 1.6 fusion.55
  56.2 1.6 fusion.57
  57.8 0.4 fusion.56
  58.3 1.6 fusion.55
  59.9 1.6 fusion.57
  62.0 1.6 fusion.55
  63.6 1.6 fusion.57
  65.7 1.6 fusion.55
  67.3 1.6 fusion.57
  69.4 1.6 fusion.55
  71.0 1.6 fusion.57
  73.1 1.6 fusion.55
  74.6 1.6 fusion.57
  76.7 1.6 fusion.55
  78.3 1.6 fusion.57
  80.4 1.6 fusion.55
  82.0 1.6 fusion.57
  84.5 12.0 %scatter_fusion = f32[32,8,8]{2,1,0:T(8,128)S(1)} fusion(f32[32,8,8]{2,1,0:T(8,128)S(1)} %broadcast_in_dim.110, s32[256]{0:T(256)S(1)} %reshape.167, f32[256,8]{1,0:T(8,128)S(1)} %bitcast.98), kind=kCustom, calls=%fused_computation.2 | custom fusion | flops 2048 | bytes 26624 | tf_op jit(solution)/shard_map/scatter-max | solution.py:29
  96.5 37.2 %pmax.7 = bf16[32,8,8]{2,1,0:T(8,128)(2,1)S(1)} all-reduce(bf16[32,8,8]{2,1,0:T(8,128)(2,1)S(1)} %convert_element_type.80), channel_id=1, replica_groups=mesh['ctx'=8,'mp'=4] {'ctx','mp'}, use_global_device_ids=true, to_apply=%region_12.13 | all-reduce | flops 2048 | bytes 8192 | tf_op jit(solution)/shard_map/pmax | solution.py:32
  133.8 1.4 gather_fusion.1
  136.0 0.9 multiply_convert_fusion
  136.9 6.1 %all-to-all-start = ((bf16[8,32,1024]{2,1,0:T(8,128)(2,1)}), bf16[8,32,1024]{2,1,0:T(8,128)(2,1)S(1)}, u32[]{:S(2)}, u32[]{:S(2)}) async-start(bf16[8,32,1024]{2,1,0:T(8,128)(2,1)} %multiply_convert_fusion), calls=%async_computation | async-start | bytes 1048576 | tf_op jit(solution)/shard_map/all_to_all | solution.py:107
  143.1 0.7 dynamic-slice_bitcast_fusion
  144.3 11.5 %all-to-all-done = bf16[8,32,1024]{2,1,0:T(8,128)(2,1)S(1)} async-done(((bf16[8,32,1024]{2,1,0:T(8,128)(2,1)}), bf16[8,32,1024]{2,1,0:T(8,128)(2,1)S(1)}, u32[]{:S(2)}, u32[]{:S(2)}) %all-to-all-start) | async-done | bytes 524320 | tf_op jit(solution)/shard_map/all_to_all | solution.py:107
  155.8 2.7 scatter_custom_fusion.1
  158.5 0.6 convert_element_type.84
  159.4 9.9 %all_to_all.10 = bf16[8,2,128]{2,1,0:T(2,128)(2,1)S(1)} all-to-all(bf16[8,2,128]{2,1,0:T(2,128)(2,1)S(1)} %reshape.200), channel_id=1, replica_groups=mesh['ctx'=8,'mp'=4] {'ctx'}, dimensions={0} | all-to-all | bytes 8192 | tf_op jit(solution)/shard_map/all_to_all | solution.py:110
  169.5 1.8 scatter_custom_fusion.2
  171.3 6.0 %psum.29 = bf16[32,8]{1,0:T(8,128)(2,1)S(1)} all-reduce(bf16[32,8]{1,0:T(8,128)(2,1)S(1)} %convert_element_type.88), channel_id=1, replica_groups=mesh['ctx'=8,'mp'=4] {'mp'}, use_global_device_ids=true, to_apply=%region_16.17 | all-reduce | flops 256 | bytes 1024 | tf_op jit(solution)/shard_map/psum | solution.py:118
  177.4 12.6 %all-reduce.7.cloned.1.call-done = bf16[32,1024]{1,0:T(8,128)(2,1)} async-done(((bf16[32,1024]{1,0:T(8,128)(2,1)}), bf16[32,1024]{1,0:T(8,128)(2,1)}) %all-reduce.7.cloned.1.call-update) | async-done | bytes 65552 | tf_op jit(solution)/shard_map/psum | solution.py:117
  190.0 3.7 fusion.25
  193.8 0.6 dynamic-slice
  195.1 69.9 %all-reduce.11.cloned.1.call-done = f32[32,2048]{1,0:T(8,128)} async-done(((f32[32,2048]{1,0:T(8,128)}), f32[32,2048]{1,0:T(8,128)}) %all-reduce.11.cloned.1.call-update) | async-done | bytes 262160
  265.0 1.0 fusion.28
  266.0 5.7 %psum.30 = f32[4]{0:T(128)S(1)} all-reduce(f32[4]{0:T(128)S(1)} %get-tuple-element.58), channel_id=1, replica_groups=mesh['ctx'=8,'mp'=4] {'mp'}, use_global_device_ids=true, to_apply=%region_19.20 | all-reduce | flops 4 | bytes 32 | tf_op jit(solution)/shard_map/psum | solution.py:134
  271.7 30.8 %all-gather = bf16[8,4,2048]{2,1,0:T(4,128)(2,1)S(1)} all-gather(bf16[1,4,2048]{2,1,0:T(4,128)(2,1)S(1)} %fusion.32), channel_id=1, replica_groups=mesh['ctx'=8,'mp'=4] {'ctx'}, dimensions={0}, use_global_device_ids=true | all-gather | bytes 147456 | tf_op jit(solution)/shard_map/all_gather | solution.py:138
  302.5 4.6 %fusion.13 = bf16[32,1,1792]{2,0,1:T(8,128)(2,1)S(1)} fusion(bf16[32,2048]{1,0:T(8,128)(2,1)S(1)} %reshape.193, bf16[2048,1792]{1,0:T(8,128)(2,1)} %param.19), kind=kOutput, calls=%fused_computation.22 | convolution fusion | flops 234938368 | bytes 7585792 | tf_op jit(solution)/shard_map/dot_general | solution.py:139
  307.1 1.3 fusion.14
  308.5 0.7 pad_maximum_fusion
  309.2 31.7 %all-reduce.9.cloned.1.call-done = bf16[32,2,1792]{2,0,1:T(8,128)(2,1)} async-done(((bf16[32,2,1792]{2,0,1:T(8,128)(2,1)}), bf16[32,2,1792]{2,0,1:T(8,128)(2,1)}) %all-reduce.9.cloned.1.call-update) | async-done | bytes 229392 | tf_op jit(solution)/shard_map/psum | solution.py:142
  340.9 1.0 convert_element_type.94
  341.9 4.4 %fusion.22 = f32[32,2048]{1,0:T(8,128)S(1)} fusion(bf16[1792,2048]{1,0:T(8,128)(2,1)} %param.21, f32[32,2,1792]{2,0,1:T(8,128)S(1)} %convert_element_type.94), kind=kOutput, calls=%fused_computation.42 | convolution fusion | flops 235225088 | bytes 8060928 | tf_op jit(solution)/shard_map/dot_general | solution.py:146
  346.3 40.2 %all-reduce.12 = bf16[32,2048]{1,0:T(8,128)(2,1)S(1)} all-reduce(f32[32,2048]{1,0:T(8,128)S(1)} %fusion.22), channel_id=3, replica_groups=mesh['ctx'=8,'mp'=4] {'ctx'}, use_global_device_ids=true, to_apply=%region_21.22.clone | all-reduce | flops 65536 | bytes 393216
  386.5 0.6 dynamic-slice_convert_fusion
  (81 shorter events, 6.8 us)
Async XLA Ops:
  136.9 56.9 %copy-start.3 = (u32[32]{0:T(128)S(1)}, u32[32]{0:T(128)}, u32[]{:S(2)}) copy-start(u32[32]{0:T(128)} %constant.135) | copy-start | bytes 388
  136.9 128.0 %copy-start.1 = (bf16[4,2048]{1,0:T(4,128)(2,1)S(1)}, bf16[4,2048]{1,0:T(4,128)(2,1)}, u32[]{:S(2)}) copy-start(bf16[4,2048]{1,0:T(4,128)(2,1)} %param.16) | copy-start | bytes 49156
  136.9 134.7 %copy-start.2 = (f32[2048]{0:T(1024)S(1)}, f32[2048]{0:T(1024)}, u32[]{:S(2)}) copy-start(f32[2048]{0:T(1024)} %param.18) | copy-start | bytes 24580
  136.9 18.8 %all-to-all-start = ((bf16[8,32,1024]{2,1,0:T(8,128)(2,1)}), bf16[8,32,1024]{2,1,0:T(8,128)(2,1)S(1)}, u32[]{:S(2)}, u32[]{:S(2)}) async-start(bf16[8,32,1024]{2,1,0:T(8,128)(2,1)} %multiply_convert_fusion), calls=%async_computation | async-start | bytes 1048576 | tf_op jit(solution)/shard_map/all_to_all | solution.py:107
  143.0 46.9 %all-reduce.7.cloned.1.call-start = ((), (), s32[]{:S(2)}) async-start(), calls=%async_computation.2 | async-start | bytes 131072 | tf_op jit(solution)/shard_map/psum | solution.py:117
  159.2 105.8 %all-reduce.11.cloned.1.call-start = ((), (), s32[]{:S(2)}) async-start(), calls=%async_computation.4 | async-start | bytes 524288
  171.3 135.8 %slice-start = ((s8[7340032]{0:T(1024)(128)(4,1)}), s8[3145728]{0:T(1024)(128)(4,1)S(1)}, s32[]{:S(2)}) async-start(s8[7340032]{0:T(1024)(128)(4,1)} %bitcast.92), calls=%async_computation.5 | async-start | bytes 6291456
  193.8 147.1 %all-reduce.9.cloned.1.call-start = ((), (), s32[]{:S(2)}) async-start(), calls=%async_computation.3 | async-start | bytes 458752 | tf_op jit(solution)/shard_map/psum | solution.py:142
  266.0 42.5 %copy-start = (bf16[4,2048]{1,0:T(4,128)(2,1)}, bf16[4,2048]{1,0:T(4,128)(2,1)S(1)}, u32[]{:S(2)}) copy-start(bf16[4,2048]{1,0:T(4,128)(2,1)S(1)} %get-tuple-element.59) | copy-start | bytes 49156
  302.5 4.6 %slice-start.1 = ((s8[7340032]{0:T(1024)(128)(4,1)}), s8[4194304]{0:T(1024)(128)(4,1)S(1)}, s32[]{:S(2)}) async-start(s8[7340032]{0:T(1024)(128)(4,1)} %bitcast.92), calls=%async_computation.6 | async-start | bytes 8388608
Sparse Core Ops, SparseCore 0:
  159.3 30.5 all-reduce.6
  193.9 71.0 all-reduce.10
  309.3 31.5 all-reduce.8
where the time goes:
time: 395 us; the launch traced here: 394 us
  blocking collectives  175 us (44%)
  waiting for transfers between devices  126 us (32%)
  matrix products  39.2 us (10%)
  other arithmetic  26.3 us (7%)
  between operations  14.7 us (4%)
  local copies, waits for them, and re-layouts  6.66 us (2%)
  starting transfers between devices  6.18 us (2%)
    unnamed x4, waiting for transfers between devices  69.9 us
    all_gather x1, blocking collectives, per_device(): all_queries = lax.all_gather(query, ('ctx', 'mp'), axis=0, tiled=True)  44.9 us
    unnamed x1, blocking collectives  40.2 us
    pmax x1, blocking collectives, global_scaling(): lax.pmax(max_table.astype(jnp.bfloat16), ('ctx', 'mp'))  37.2 us
    psum x1, waiting for transfers between devices, per_device(): gate_up = lax.psum(gate_up.astype(jnp.bfloat16), 'mp').astype(jnp.float32)  31.7 us
    all_gather x1, blocking collectives, per_device(): row_piece = lax.all_gather(normed, 'ctx', axis=0, tiled=True)  30.8 us
    dot_general x8, matrix products, attend(): jnp.dot(probs.astype(jnp.bfloat16), value_block, preferred_element_type=j...  12.6 us
    psum x1, waiting for transfers between devices, per_device(): lax.psum(numerator.astype(jnp.bfloat16), 'mp').astype(jnp.float32)  12.6 us
  transfers between devices with their start and end apart: 4, of which 4 were waited for; matrix products, arithmetic and copies ran while one was open for 1% of the time, Pallas kernels for 0%

commit v1 on v0

--- a/solution.py
+++ b/solution.py
@@ -8,6 +8,12 @@
 ROW_DEV = 1
 norm_eps = 1e-05
 lowest_value = -1e30
+
+
+def add_all(x, mesh_axis):
+    shards = lax.all_gather(x, mesh_axis, axis=0, tiled=False)
+    total = shards.sum(axis=0)
+    return total
 
 
 def find_slots(listed, target, capacity):
@@ -139,7 +145,7 @@
     gate_piece = jnp.dot(row_piece, gate_weight, preferred_element_type=jnp.float32)
     up_piece = jnp.dot(row_piece, up_weight, preferred_element_type=jnp.float32)
     gate_up = jnp.stack([gate_piece, up_piece], axis=1)
-    gate_up = lax.psum(gate_up.astype(jnp.bfloat16), "mp").astype(jnp.float32)
+    gate_up = add_all(gate_up.astype(jnp.bfloat16), "mp").astype(jnp.float32)
     hidden = (jax.nn.silu(gate_up[:, 0]) * gate_up[:, 1]).astype(jnp.bfloat16)
     rows_here = hidden
     update = lax.psum_scatter(

time: 395 us -> 370 us (0.937)
  waiting for transfers between devices: 126 us -> 94 us
  blocking collectives: 175 us -> 182 us
    psum x1 -> x0, waiting for transfers between devices: 31.7 us -> none  [per_device(): gate_up = lax.psum(gate_up.astype(jnp.bfloat16), 'mp').astype(jnp.float32)]
    all_gather x0 -> x1, blocking collectives: none -> 9.5 us  [add_all(): shards = lax.all_gather(x, mesh_axis, axis=0, tiled=False)]
    unnamed x4 -> x3, waiting for transfers between devices: 69.9 us -> 70 us
  transfers between devices with their start and end apart: 4 -> 3, of which waited for: 4 -> 3; matrix products, arithmetic and copies ran while one was open for 1% -> 1% of each run, Pallas kernels for 0% -> 0%
where the time goes in v1:
time: 370 us; the launch traced here: 369 us
  blocking collectives  182 us (49%)
  waiting for transfers between devices  94 us (25%)
  matrix products  39.1 us (11%)
  other arithmetic  24.8 us (7%)
  between operations  15 us (4%)
  local copies, waits for them, and re-layouts  6.66 us (2%)
  starting transfers between devices  6.13 us (2%)
    unnamed x3, waiting for transfers between devices  70 us
    all_gather x1, blocking collectives, per_device(): all_queries = lax.all_gather(query, ('ctx', 'mp'), axis=0, tiled=True)  44.9 us
    unnamed x1, blocking collectives  38.4 us
    pmax x1, blocking collectives, global_scaling(): lax.pmax(max_table.astype(jnp.bfloat16), ('ctx', 'mp'))  37.2 us
    all_gather x1, blocking collectives, per_device(): row_piece = lax.all_gather(normed, 'ctx', axis=0, tiled=True)  30.8 us
    dot_general x8, matrix products, attend(): jnp.dot(probs.astype(jnp.bfloat16), value_block, preferred_element_type=j...  12.6 us
    psum x1, waiting for transfers between devices, per_device(): lax.psum(numerator.astype(jnp.bfloat16), 'mp').astype(jnp.float32)  12.6 us
    dot_general x8, matrix products, attend(): lax.dot_general(query_block, key_block, (((1,), (1,)), ((), ())), preferr...  12.5 us
  transfers between devices with their start and end apart: 3, of which 3 were waited for; matrix products, arithmetic and copies ran while one was open for 1% of the time, Pallas kernels for 0%

profile of v1, /device:TPU:0, one launch (start us, length us, event | category | flops | bytes accessed | tf_op | source)
XLA Modules:
  0.0 368.6 jit_solution(12747950885445134333)
XLA Ops:
  7.2 0.9 compare_reduce_fusion
  8.6 44.9 %all_gather.10 = bf16[32,8,8,128]{3,2,1,0:T(8,128)(2,1)S(1)} all-gather(bf16[1,8,8,128]{3,2,1,0:T(8,128)(2,1)} %param.12), channel_id=1, replica_groups=mesh['ctx'=8,'mp'=4] {'ctx','mp'}, dimensions={0}, use_global_device_ids=true | all-gather | bytes 540672 | tf_op jit(solution)/shard_map/all_gather | solution.py:69
  53.5 1.1 gather_fusion
  54.7 29.4 %while.14 = (s32[]{:T(128)}, f32[8,256]{1,0:T(8,128)S(1)}, f32[8,256]{1,0:T(8,128)S(1)}, f32[8,256,128]{2,1,0:T(8,128)S(1)}, bf16[8,256,128]{2,1,0:T(8,128)(2,1)...) while((s32[]{:T(128)}, f32[8,256]{1,0:T(8,128)S(1)}, ...), condition=%wide.region_9.10_spmd, body=%wide.region_6.9_spmd.sunk | while | flops 271580672 | bytes 7546981 | solution.py:94
  54.7 1.6 fusion.55
  56.2 1.6 fusion.57
  57.8 0.4 fusion.56
  58.3 1.6 fusion.55
  59.9 1.6 fusion.57
  61.5 0.4 fusion.56
  62.0 1.6 fusion.55
  63.6 1.6 fusion.57
  65.2 0.4 fusion.56
  65.7 1.6 fusion.55
  67.3 1.6 fusion.57
  69.4 1.6 fusion.55
  71.0 1.6 fusion.57
  73.1 1.6 fusion.55
  74.6 1.6 fusion.57
  76.7 1.6 fusion.55
  78.3 1.6 fusion.57
  80.4 1.6 fusion.55
  82.0 1.6 fusion.57
  84.5 12.0 %scatter_fusion = f32[32,8,8]{2,1,0:T(8,128)S(1)} fusion(f32[32,8,8]{2,1,0:T(8,128)S(1)} %broadcast_in_dim.110, s32[256]{0:T(256)S(1)} %reshape.200, f32[256,8]{1,0:T(8,128)S(1)} %bitcast.98), kind=kCustom, calls=%fused_computation.2 | custom fusion | flops 2048 | bytes 26624 | tf_op jit(solution)/shard_map/scatter-max | solution.py:35
  96.5 37.2 %pmax.7 = bf16[32,8,8]{2,1,0:T(8,128)(2,1)S(1)} all-reduce(bf16[32,8,8]{2,1,0:T(8,128)(2,1)S(1)} %convert_element_type.89), channel_id=1, replica_groups=mesh['ctx'=8,'mp'=4] {'ctx','mp'}, use_global_device_ids=true, to_apply=%region_12.13 | all-reduce | flops 2048 | bytes 8192 | tf_op jit(solution)/shard_map/pmax | solution.py:38
  133.8 1.4 gather_fusion.1
  136.0 0.9 multiply_convert_fusion
  137.0 6.1 %all-to-all-start = ((bf16[8,32,1024]{2,1,0:T(8,128)(2,1)}), bf16[8,32,1024]{2,1,0:T(8,128)(2,1)S(1)}, u32[]{:S(2)}, u32[]{:S(2)}) async-start(bf16[8,32,1024]{2,1,0:T(8,128)(2,1)} %multiply_convert_fusion), calls=%async_computation | async-start | bytes 1048576 | tf_op jit(solution)/shard_map/all_to_all | solution.py:113
  143.1 0.7 dynamic-slice_bitcast_fusion
  144.3 11.5 %all-to-all-done = bf16[8,32,1024]{2,1,0:T(8,128)(2,1)S(1)} async-done(((bf16[8,32,1024]{2,1,0:T(8,128)(2,1)}), bf16[8,32,1024]{2,1,0:T(8,128)(2,1)S(1)}, u32[]{:S(2)}, u32[]{:S(2)}) %all-to-all-start) | async-done | bytes 524320 | tf_op jit(solution)/shard_map/all_to_all | solution.py:113
  155.8 2.7 scatter_custom_fusion.1
  158.5 0.6 convert_element_type.93
  159.4 9.9 %all_to_all.10 = bf16[8,2,128]{2,1,0:T(2,128)(2,1)S(1)} all-to-all(bf16[8,2,128]{2,1,0:T(2,128)(2,1)S(1)} %reshape.233), channel_id=1, replica_groups=mesh['ctx'=8,'mp'=4] {'ctx'}, dimensions={0} | all-to-all | bytes 8192 | tf_op jit(solution)/shard_map/all_to_all | solution.py:116
  169.5 1.8 scatter_custom_fusion.2
  171.3 6.0 %psum.22 = bf16[32,8]{1,0:T(8,128)(2,1)S(1)} all-reduce(bf16[32,8]{1,0:T(8,128)(2,1)S(1)} %convert_element_type.97), channel_id=1, replica_groups=mesh['ctx'=8,'mp'=4] {'mp'}, use_global_device_ids=true, to_apply=%region_16.17 | all-reduce | flops 256 | bytes 1024 | tf_op jit(solution)/shard_map/psum | solution.py:124
  177.4 12.6 %all-reduce.6.cloned.1.call-done = bf16[32,1024]{1,0:T(8,128)(2,1)} async-done(((bf16[32,1024]{1,0:T(8,128)(2,1)}), bf16[32,1024]{1,0:T(8,128)(2,1)}) %all-reduce.6.cloned.1.call-update) | async-done | bytes 65552 | tf_op jit(solution)/shard_map/psum | solution.py:123
  190.0 3.7 %fusion.25 = f32[32,2048]{1,0:T(8,128)} fusion(bf16[1024,2048]{1,0:T(8,128)(2,1)} %param.17, f32[4,8,8,128]{3,2,1,0:T(8,128)S(1)} %bitcast.99, bf16[32,1024]{1,0:T(8,128)(2,1)} %all-reduce.6.cloned.1.call-done), kind=kOutput, calls=%fused_computation.44 | convolution fusion | flops 134316032 | bytes 4653056 | tf_op jit(solution)/shard_map/dot_general | solution.py:133
  193.8 0.6 dynamic-slice
  195.0 69.9 %all-reduce.8.cloned.1.call-done = f32[32,2048]{1,0:T(8,128)} async-done(((f32[32,2048]{1,0:T(8,128)}), f32[32,2048]{1,0:T(8,128)}) %all-reduce.8.cloned.1.call-update) | async-done | bytes 262160
  265.0 1.0 fusion.28
  266.0 5.7 %psum.23 = f32[4]{0:T(128)S(1)} all-reduce(f32[4]{0:T(128)S(1)} %get-tuple-element.58), channel_id=1, replica_groups=mesh['ctx'=8,'mp'=4] {'mp'}, use_global_device_ids=true, to_apply=%region_19.20 | all-reduce | flops 4 | bytes 32 | tf_op jit(solution)/shard_map/psum | solution.py:140
  271.7 30.8 %all-gather = bf16[8,4,2048]{2,1,0:T(4,128)(2,1)S(1)} all-gather(bf16[1,4,2048]{2,1,0:T(4,128)(2,1)S(1)} %fusion.32), channel_id=1, replica_groups=mesh['ctx'=8,'mp'=4] {'ctx'}, dimensions={0}, use_global_device_ids=true | all-gather | bytes 147456 | tf_op jit(solution)/shard_map/all_gather | solution.py:144
  302.5 4.6 %fusion.13 = bf16[1,32,1,1792]{3,1,2,0:T(8,128)(2,1)S(1)} fusion(bf16[32,2048]{1,0:T(8,128)(2,1)S(1)} %reshape.226, bf16[2048,1792]{1,0:T(8,128)(2,1)} %param.19), kind=kOutput, calls=%fused_computation.22 | convolution fusion | flops 234938368 | bytes 7585792 | tf_op jit(solution)/shard_map/dot_general | solution.py:145
  307.1 1.3 fusion.14
  308.5 9.5 %all_gather.12 = bf16[4,32,2,1792]{3,1,2,0:T(8,128)(2,1)S(1)} all-gather(bf16[1,32,2,1792]{3,1,2,0:T(8,128)(2,1)S(1)} %pad_maximum_fusion), channel_id=1, replica_groups=mesh['ctx'=8,'mp'=4] {'mp'}, dimensions={0}, use_global_device_ids=true | all-gather | bytes 1146880 | tf_op jit(solution)/shard_map/all_gather | solution.py:14
  318.2 4.4 %fusion.22 = f32[32,2048]{1,0:T(8,128)S(1)} fusion(bf16[1792,2048]{1,0:T(8,128)(2,1)} %param.21, f32[32,2,1792]{2,0,1:T(8,128)S(1)} %convert_element_type.103), kind=kOutput, calls=%fused_computation.42 | convolution fusion | flops 235225088 | bytes 8060928 | tf_op jit(solution)/shard_map/dot_general | solution.py:152
  322.6 38.4 %all-reduce.9 = bf16[32,2048]{1,0:T(8,128)(2,1)S(1)} all-reduce(f32[32,2048]{1,0:T(8,128)S(1)} %fusion.22), channel_id=3, replica_groups=mesh['ctx'=8,'mp'=4] {'ctx'}, use_global_device_ids=true, to_apply=%region_21.22.clone | all-reduce | flops 65536 | bytes 393216
  361.1 0.6 dynamic-slice_convert_fusion
  (80 shorter events, 6.1 us)
Async XLA Ops:
  136.9 56.8 %copy-start.3 = (u32[32]{0:T(128)S(1)}, u32[32]{0:T(128)}, u32[]{:S(2)}) copy-start(u32[32]{0:T(128)} %constant.137) | copy-start | bytes 388
  136.9 128.0 %copy-start.1 = (bf16[4,2048]{1,0:T(4,128)(2,1)S(1)}, bf16[4,2048]{1,0:T(4,128)(2,1)}, u32[]{:S(2)}) copy-start(bf16[4,2048]{1,0:T(4,128)(2,1)} %param.16) | copy-start | bytes 49156
  137.0 134.7 %copy-start.2 = (f32[2048]{0:T(1024)S(1)}, f32[2048]{0:T(1024)}, u32[]{:S(2)}) copy-start(f32[2048]{0:T(1024)} %param.18) | copy-start | bytes 24580
  137.0 18.8 %all-to-all-start = ((bf16[8,32,1024]{2,1,0:T(8,128)(2,1)}), bf16[8,32,1024]{2,1,0:T(8,128)(2,1)S(1)}, u32[]{:S(2)}, u32[]{:S(2)}) async-start(bf16[8,32,1024]{2,1,0:T(8,128)(2,1)} %multiply_convert_fusion), calls=%async_computation | async-start | bytes 1048576 | tf_op jit(solution)/shard_map/all_to_all | solution.py:113
  143.0 46.9 %all-reduce.6.cloned.1.call-start = ((), (), s32[]{:S(2)}) async-start(), calls=%async_computation.2 | async-start | bytes 131072 | tf_op jit(solution)/shard_map/psum | solution.py:123
  159.2 105.8 %all-reduce.8.cloned.1.call-start = ((), (), s32[]{:S(2)}) async-start(), calls=%async_computation.3 | async-start | bytes 524288
  171.3 135.8 %slice-start = ((s8[7340032]{0:T(1024)(128)(4,1)}), s8[3145728]{0:T(1024)(128)(4,1)S(1)}, s32[]{:S(2)}) async-start(s8[7340032]{0:T(1024)(128)(4,1)} %bitcast.92), calls=%async_computation.4 | async-start | bytes 6291456
  265.9 42.5 %copy-start = (bf16[4,2048]{1,0:T(4,128)(2,1)}, bf16[4,2048]{1,0:T(4,128)(2,1)S(1)}, u32[]{:S(2)}) copy-start(bf16[4,2048]{1,0:T(4,128)(2,1)S(1)} %get-tuple-element.59) | copy-start | bytes 49156
  302.5 4.6 %slice-start.1 = ((s8[7340032]{0:T(1024)(128)(4,1)}), s8[4194304]{0:T(1024)(128)(4,1)S(1)}, s32[]{:S(2)}) async-start(s8[7340032]{0:T(1024)(128)(4,1)} %bitcast.92), calls=%async_computation.5 | async-start | bytes 8388608
Sparse Core Ops, SparseCore 0:
  159.3 30.5 all-reduce.5
  193.9 71.0 all-reduce.7
